TPU v7x, 32 devices: a whole 2x2x4 slice. The times are simulated.
32 devices in a mesh: dp: 4 (over x, core), gx: 2 (over y), gy: 4 (over z).
Axes of the slice: x: 2, y: 2, z: 4, core: 2. Of those that a mesh axis runs over, the one named last changes fastest.
Arguments:
- inputs: bfloat16 [4096, 960], P(('dp', 'gx', 'gy')), may hold values from -6 to 6
- segments: int32 [4096], P('dp'), may hold values from 0 to 15, never falling along the last dimension, each value on 1 to 512 neighbouring positions
- attn_gain: float32 [960], replicated, may hold values from 0.5 to 1.5
- query_weight: bfloat16 [960, 960], P('gx', 'gy'), may hold values from -1.6 to 1.6
- key_weight: bfloat16 [960, 320], P('gx', 'gy'), may hold values from -1.6 to 1.6
- value_weight: bfloat16 [960, 320], P('gx', 'gy'), may hold values from -0.1875 to 0.1875
- output_weight: bfloat16 [960, 960], P('gx', 'gy'), may hold values from -0.75 to 0.75
- mlp_gain: float32 [960], replicated, may hold values from 0.5 to 1.5
- gate_weight: bfloat16 [960, 2560], P('gx', 'gy'), may hold values from -0.1875 to 0.1875
- up_weight: bfloat16 [960, 2560], P('gx', 'gy'), may hold values from -0.1875 to 0.1875
- down_weight: bfloat16 [2560, 960], P('gx', 'gy'), may hold values from -0.125 to 0.125
- cotangent: bfloat16 [4096, 960], P(('dp', 'gx', 'gy')), may hold values from -6 to 6
Outputs:
- layer_out: bfloat16 [4096, 960], P(('dp', 'gx', 'gy'))
- input_grad: bfloat16 [4096, 960], P(('dp', 'gx', 'gy'))
- query_grad: float32 [960, 960], P('gx', 'gy')
- key_grad: float32 [960, 320], P('gx', 'gy')
- value_grad: float32 [960, 320], P('gx', 'gy')
- output_grad: float32 [960, 960], P('gx', 'gy')
- gate_grad: float32 [960, 2560], P('gx', 'gy')
- up_grad: float32 [960, 2560], P('gx', 'gy')
- down_grad: float32 [2560, 960], P('gx', 'gy')
- attgain_grad: float32 [960], replicated
- mlpgain_grad: float32 [960], replicated
Inputs may be any that keep to these rules, and one draw needn't show every extreme that they name: `segments`: segment numbers never fall along the tokens; a document may run on past the end of a sequence.
All inputs are finite; a program needn't handle non-finite values.
Results may differ from a plain program's by a relative error of at most 0.04.
Values may be sent and summed in bfloat16 or wider, within the bound.
A program may use at most 128 MiB of HBM per device.

v0:
```python
import jax
import jax.numpy as jnp
from jax import lax
from jax.sharding import PartitionSpec as P

QUERY_HEADS = 15
KEY_VALUE_HEADS = 5
HEAD_WIDTH = 64
SEQUENCE_LENGTH = 1024
THETA = 100000.0
EPSILON = 1e-05
MASKED = -1e30


def rope_angles(positions):
    half_dim = HEAD_WIDTH // 2
    inverse = THETA ** (-(jnp.arange(half_dim, dtype=jnp.float32) * 2.0 / HEAD_WIDTH))
    angles = positions[:, None] * inverse[None, :]
    return (jnp.cos(angles)[:, None, :], jnp.sin(angles)[:, None, :])


def rotate(values, cos_table, sin_table):
    item_count = values.shape[0]
    shaped = values.reshape(item_count, -1, HEAD_WIDTH)
    half_dim = HEAD_WIDTH // 2
    front_part = shaped[:, :, :half_dim]
    back_part = shaped[:, :, half_dim:]
    turned = jnp.concatenate(
        [
            front_part * cos_table - back_part * sin_table,
            back_part * cos_table + front_part * sin_table,
        ],
        axis=2,
    )
    return turned.reshape(item_count, -1)


def unrotate(values, cos_table, sin_table):
    item_count = values.shape[0]
    shaped = values.reshape(item_count, -1, HEAD_WIDTH)
    half_dim = HEAD_WIDTH // 2
    front_part = shaped[:, :, :half_dim]
    back_part = shaped[:, :, half_dim:]
    turned = jnp.concatenate(
        [
            front_part * cos_table + back_part * sin_table,
            back_part * cos_table - front_part * sin_table,
        ],
        axis=2,
    )
    return turned.reshape(item_count, -1)


def normalize(values, gain):
    rms_rows = lax.rsqrt(jnp.mean(values * values, axis=1, keepdims=True) + EPSILON)
    unit_rows = values * rms_rows
    return (rms_rows, unit_rows, (unit_rows * gain).astype(jnp.bfloat16))


def normalize_back(dnormed, gain, rms_rows, unit_rows):
    scaled = dnormed * gain
    dvalues = rms_rows * (scaled - unit_rows * jnp.mean(scaled * unit_rows, axis=1, keepdims=True))
    return (dvalues, jnp.sum(dnormed * unit_rows, axis=0))


def weight_product(left, right):
    return lax.dot_general(
        left, right, (((0,), (0,)), ((), ())), preferred_element_type=jnp.float32
    )


def back_product(left, right):
    return lax.dot_general(
        left, right, (((1,), (1,)), ((), ())), preferred_element_type=jnp.float32
    )


def gather_blocks(block):
    return lax.all_gather(block, ("gx", "gy"), axis=0, tiled=False)


def whole_weight(blocks):
    fanin = lax.axis_size("gx")
    fanout = lax.axis_size("gy")
    rows, columns = blocks.shape[1:]
    shaped = blocks.reshape(fanin, fanout, rows, columns).transpose(0, 2, 1, 3)
    return shaped.reshape(fanin * rows, fanout * columns)


def cut_blocks(grad):
    fanin = lax.axis_size("gx")
    fanout = lax.axis_size("gy")
    rows, columns = (grad.shape[0] // fanin, grad.shape[1] // fanout)
    shaped = grad.astype(jnp.bfloat16).reshape(fanin, rows, fanout, columns).transpose(0, 2, 1, 3)
    return shaped.reshape(fanin * fanout, rows, columns)


def scatter_blocks(blocks):
    return lax.psum_scatter(blocks, ("gx", "gy"), scatter_dimension=0, tiled=False)


def hidden_slice(weight, groups):
    rows, columns = weight.shape
    share = rows // groups // lax.axis_size("dp")
    shaped = weight.reshape(groups, lax.axis_size("dp"), share, columns)
    picked = lax.dynamic_slice_in_dim(shaped, lax.axis_index("dp"), 1, 1)
    return picked.reshape(groups * share, columns)


def head_views(rotated_query, key_sequence, value_sequence):
    query_groups = QUERY_HEADS // KEY_VALUE_HEADS
    query_head_split = rotated_query.reshape(
        rotated_query.shape[0], KEY_VALUE_HEADS, query_groups, HEAD_WIDTH
    )
    key_head_split = key_sequence.reshape(key_sequence.shape[0], KEY_VALUE_HEADS, HEAD_WIDTH)
    value_head_split = value_sequence.reshape(value_sequence.shape[0], KEY_VALUE_HEADS, HEAD_WIDTH)
    return (query_head_split, key_head_split, value_head_split)


def masked_scores(query_head_split, key_head_split, allowed):
    scores = jnp.einsum(
        "tkgd,ukd->kgtu", query_head_split, key_head_split, preferred_element_type=jnp.float32
    ) * HEAD_WIDTH ** (-0.5)
    return jnp.where(allowed, scores, MASKED)


def attend(rotated_query, key_sequence, value_sequence, allowed):
    query_head_split, key_head_split, value_head_split = head_views(
        rotated_query, key_sequence, value_sequence
    )
    scores = masked_scores(query_head_split, key_head_split, allowed)
    highest = jnp.max(scores, axis=3, keepdims=True)
    logsum = highest + jnp.log(jnp.sum(jnp.exp(scores - highest), axis=3, keepdims=True))
    probs = jnp.exp(scores - logsum).astype(jnp.bfloat16)
    attention_mixture = jnp.einsum(
        "kgtu,ukd->tkgd", probs, value_head_split, preferred_element_type=jnp.float32
    )
    return (attention_mixture.reshape(rotated_query.shape[0], -1).astype(jnp.bfloat16), logsum)


def attend_back(
    rotated_query,
    key_sequence,
    value_sequence,
    allowed,
    logsum,
    attention_mixture,
    mixture_gradient,
):
    query_head_split, key_head_split, value_head_split = head_views(
        rotated_query, key_sequence, value_sequence
    )
    count_of_rows = rotated_query.shape[0]
    query_groups = QUERY_HEADS // KEY_VALUE_HEADS
    soft_weights = jnp.exp(masked_scores(query_head_split, key_head_split, allowed) - logsum)
    probs = soft_weights.astype(jnp.bfloat16)
    mixture_head_gradient = mixture_gradient.reshape(
        count_of_rows, KEY_VALUE_HEADS, query_groups, HEAD_WIDTH
    )
    mixture_heads = attention_mixture.reshape(
        count_of_rows, KEY_VALUE_HEADS, query_groups, HEAD_WIDTH
    )
    row_delta = jnp.sum(
        mixture_heads.astype(jnp.float32) * mixture_head_gradient.astype(jnp.float32), axis=3
    )
    row_delta = jnp.transpose(row_delta, (1, 2, 0))[:, :, :, None]
    dprobs = jnp.einsum(
        "tkgd,ukd->kgtu",
        mixture_head_gradient,
        value_head_split,
        preferred_element_type=jnp.float32,
    )
    dscores = (soft_weights * (dprobs - row_delta)).astype(jnp.bfloat16)
    dquery = jnp.einsum(
        "kgtu,ukd->tkgd", dscores, key_head_split, preferred_element_type=jnp.float32
    ).reshape(count_of_rows, -1) * HEAD_WIDTH ** (-0.5)
    dkeys = jnp.einsum(
        "kgtu,tkgd->ukd", dscores, query_head_split, preferred_element_type=jnp.float32
    ).reshape(key_sequence.shape[0], -1) * HEAD_WIDTH ** (-0.5)
    dvalues = jnp.einsum(
        "kgtu,tkgd->ukd", probs, mixture_head_gradient, preferred_element_type=jnp.float32
    ).reshape(key_sequence.shape[0], -1)
    return (dquery, dkeys, dvalues)


def on_device(
    inputs,
    segments,
    attn_gain,
    query_weight,
    key_weight,
    value_weight,
    output_weight,
    mlp_gain,
    gate_weight,
    up_weight,
    down_weight,
    cotangent,
):
    count_of_rows = inputs.shape[0]
    fanin = lax.axis_size("gx")
    fanout = lax.axis_size("gy")
    replicas = lax.axis_size("dp")
    begin_row = (lax.axis_index("gx") * fanout + lax.axis_index("gy")) * count_of_rows
    seq_begin = begin_row // SEQUENCE_LENGTH * SEQUENCE_LENGTH
    local_places = begin_row - seq_begin + jnp.arange(count_of_rows)
    cos_table, sin_table = rope_angles(local_places.astype(jnp.float32))
    query_segs = lax.dynamic_slice_in_dim(segments, begin_row, count_of_rows, 0)
    allowed = (jnp.arange(SEQUENCE_LENGTH)[None, :] <= local_places[:, None]) & (
        query_segs[:, None] == segments[None, :]
    )
    residual = inputs.astype(jnp.float32)
    rms_one, unit_one, normed_one = normalize(residual, attn_gain)
    q_width, k_width, v_width = (query_weight.shape[1], key_weight.shape[1], value_weight.shape[1])
    packed = jnp.concatenate([query_weight, key_weight, value_weight, output_weight], axis=1)
    attn_blocks = gather_blocks(packed)
    query_full = whole_weight(attn_blocks[:, :, :q_width])
    key_full = whole_weight(attn_blocks[:, :, q_width : q_width + k_width])
    value_full = whole_weight(attn_blocks[:, :, q_width + k_width : q_width + k_width + v_width])
    output_full = whole_weight(attn_blocks[:, :, q_width + k_width + v_width :])
    groups = fanout // fanin
    gate_part = hidden_slice(gate_weight.T, 1)
    up_part = hidden_slice(up_weight.T, 1)
    down_part = hidden_slice(down_weight, groups)
    share = gate_part.shape[0]
    gate_up_blocks = gather_blocks(jnp.concatenate([gate_part, up_part], axis=0))
    down_blocks = gather_blocks(down_part)
    model_block = gate_part.shape[1]
    gate_up_rows = (
        gate_up_blocks.reshape(fanin, fanout, 2, share, model_block)
        .transpose(2, 1, 3, 0, 4)
        .reshape(2 * fanout * share, fanin * model_block)
    )
    hidden_width = fanout * share
    down_rows = whole_weight(down_blocks)
    query_rows = jnp.dot(normed_one, query_full, preferred_element_type=jnp.float32).astype(
        jnp.bfloat16
    )
    key_rows = jnp.dot(normed_one, key_full, preferred_element_type=jnp.float32).astype(
        jnp.bfloat16
    )
    value_rows = jnp.dot(normed_one, value_full, preferred_element_type=jnp.float32).astype(
        jnp.bfloat16
    )
    rotated_query = rotate(query_rows.astype(jnp.float32), cos_table, sin_table).astype(
        jnp.bfloat16
    )
    rotated_key = rotate(key_rows.astype(jnp.float32), cos_table, sin_table).astype(jnp.bfloat16)
    kv_all = lax.all_gather(
        jnp.concatenate([rotated_key, value_rows], axis=1), ("gx", "gy"), axis=0, tiled=True
    )
    kv_width = rotated_key.shape[1]
    key_all, value_all = (kv_all[:, :kv_width], kv_all[:, kv_width:])
    attention_mixture, logsum = attend(rotated_query, key_all, value_all, allowed)
    attn_out = jnp.dot(attention_mixture, output_full, preferred_element_type=jnp.float32).astype(
        jnp.bfloat16
    )
    hidden = residual + attn_out.astype(jnp.float32)
    rms_two, unit_two, normed_two = normalize(hidden, mlp_gain)
    cot_all = lax.all_gather(cotangent, "dp", axis=0, tiled=True)
    normed_all = lax.all_gather(normed_two, "dp", axis=0, tiled=True)
    gate_up = back_product(normed_all, gate_up_rows).astype(jnp.bfloat16)
    gate_float = gate_up[:, :hidden_width].astype(jnp.float32)
    up_float = gate_up[:, hidden_width:].astype(jnp.float32)
    sigmoid_gate = jax.nn.sigmoid(gate_float)
    activated = (gate_float * sigmoid_gate * up_float).astype(jnp.bfloat16)
    dactivated = back_product(cot_all, down_rows)
    gate_delta = (
        dactivated * up_float * sigmoid_gate * (1.0 + gate_float * (1.0 - sigmoid_gate))
    ).astype(jnp.bfloat16)
    up_delta = (dactivated * gate_float * sigmoid_gate).astype(jnp.bfloat16)
    deltas = jnp.concatenate([gate_delta, up_delta], axis=1)
    dnormed_two = lax.psum_scatter(
        jnp.dot(deltas, gate_up_rows, preferred_element_type=jnp.float32).astype(jnp.bfloat16),
        "dp",
        scatter_dimension=0,
        tiled=True,
    ).astype(jnp.float32)
    mlp_out = lax.psum_scatter(
        jnp.dot(activated, down_rows, preferred_element_type=jnp.float32).astype(jnp.bfloat16),
        "dp",
        scatter_dimension=0,
        tiled=True,
    )
    layer_out = (hidden + mlp_out.astype(jnp.float32)).astype(jnp.bfloat16)
    gate_up_grad = (
        weight_product(deltas, normed_all)
        .astype(jnp.bfloat16)
        .reshape(2, fanout, share, fanin, model_block)
        .transpose(3, 1, 0, 2, 4)
        .reshape(fanin * fanout, 2 * share, model_block)
    )
    down_grad_blocks = cut_blocks(weight_product(activated, cot_all))
    if groups * share == 2 * share:
        mlp_sum = scatter_blocks(jnp.concatenate([gate_up_grad, down_grad_blocks], axis=2))
        mlp_sum = lax.all_gather(mlp_sum, "dp", axis=0, tiled=False)
        gate_up_sum, down_sum = (mlp_sum[:, :, :model_block], mlp_sum[:, :, model_block:])
    else:
        gate_up_sum = lax.all_gather(scatter_blocks(gate_up_grad), "dp", axis=0, tiled=False)
        down_sum = lax.all_gather(scatter_blocks(down_grad_blocks), "dp", axis=0, tiled=False)
    gate_grad = gate_up_sum[:, :share].reshape(replicas * share, model_block).T.astype(jnp.float32)
    up_grad = gate_up_sum[:, share:].reshape(replicas * share, model_block).T.astype(jnp.float32)
    down_grad = (
        down_sum.reshape(replicas, groups, share, -1)
        .transpose(1, 0, 2, 3)
        .reshape(down_weight.shape)
        .astype(jnp.float32)
    )
    dhidden_norm, mlpgain_part = normalize_back(dnormed_two, mlp_gain, rms_two, unit_two)
    dhidden = cotangent.astype(jnp.float32) + dhidden_norm
    dhidden_bf = dhidden.astype(jnp.bfloat16)
    output_sum = scatter_blocks(cut_blocks(weight_product(attention_mixture, dhidden_bf)))
    mixture_gradient = back_product(dhidden_bf, output_full).astype(jnp.bfloat16)
    dquery_rot, dkey_seq, dvalue_seq = attend_back(
        rotated_query, key_all, value_all, allowed, logsum, attention_mixture, mixture_gradient
    )
    dkv = lax.psum_scatter(
        jnp.concatenate([dkey_seq, dvalue_seq], axis=1).astype(jnp.bfloat16),
        ("gx", "gy"),
        scatter_dimension=0,
        tiled=True,
    )
    dquery = unrotate(dquery_rot, cos_table, sin_table).astype(jnp.bfloat16)
    query_sum = scatter_blocks(cut_blocks(weight_product(normed_one, dquery)))
    dkey = unrotate(dkv[:, :kv_width].astype(jnp.float32), cos_table, sin_table).astype(
        jnp.bfloat16
    )
    dvalue_bf = dkv[:, kv_width:]
    kv_sum = scatter_blocks(
        jnp.concatenate(
            [
                cut_blocks(weight_product(normed_one, dkey)),
                cut_blocks(weight_product(normed_one, dvalue_bf)),
            ],
            axis=2,
        )
    )
    dnormed_one = (
        back_product(dquery, query_full)
        + back_product(dkey, key_full)
        + back_product(dvalue_bf, value_full)
    )
    dresidual, attgain_part = normalize_back(dnormed_one, attn_gain, rms_one, unit_one)
    input_grad = (dhidden + dresidual).astype(jnp.bfloat16)
    gain_parts = lax.all_gather(
        jnp.stack([attgain_part, mlpgain_part]), ("dp", "gx", "gy"), axis=0, tiled=False
    )
    attgain_grad, mlpgain_grad = jnp.sum(gain_parts, axis=0)
    attn_sum = lax.psum(jnp.concatenate([output_sum, query_sum, kv_sum], axis=1), "dp").astype(
        jnp.float32
    )
    o_width = output_weight.shape[1]
    output_grad = attn_sum[:, :o_width]
    query_grad = attn_sum[:, o_width : o_width + q_width]
    key_grad = attn_sum[:, o_width + q_width : o_width + q_width + k_width]
    value_grad = attn_sum[:, o_width + q_width + k_width :]
    return (
        layer_out,
        input_grad,
        query_grad,
        key_grad,
        value_grad,
        output_grad,
        gate_grad,
        up_grad,
        down_grad,
        attgain_grad,
        mlpgain_grad,
    )


def solution(mesh):
    return jax.shard_map(
        on_device,
        mesh=mesh,
        in_specs=(
            P(("dp", "gx", "gy"), None),
            P("dp"),
            P(),
            P("gx", "gy"),
            P("gx", "gy"),
            P("gx", "gy"),
            P("gx", "gy"),
            P(),
            P("gx", "gy"),
            P("gx", "gy"),
            P("gx", "gy"),
            P(("dp", "gx", "gy"), None),
        ),
        out_specs=(
            P(("dp", "gx", "gy"), None),
            P(("dp", "gx", "gy"), None),
            P("gx", "gy"),
            P("gx", "gy"),
            P("gx", "gy"),
            P("gx", "gy"),
            P("gx", "gy"),
            P("gx", "gy"),
            P("gx", "gy"),
            P(),
            P(),
        ),
        check_vma=False,
    )
```

profile of v0, /device:TPU:0, one launch (start us, length us, event | category | flops | bytes accessed | tf_op | source)
XLA Modules:
  0.0 793.3 jit_solution(703122421121879821)
XLA Ops:
  9.4 2.2 pad_maximum_fusion.6
  14.5 81.8 %all-gather.16.cloned.1.call-done = bf16[3840,640]{1,0:T(8,128)(2,1)} async-done(((bf16[480,640]{1,0:T(8,128)(2,1)}), bf16[3840,640]{1,0:T(8,128)(2,1)}) %all-gather.16.cloned.1.call-update) | async-done | bytes 4915216 | tf_op jit(solution)/shard_map/all_gather | solution.py:79
  96.3 2.8 fusion.62
  104.5 10.1 %all_gather.40 = bf16[512,960]{0,1:T(8,128)(2,1)} all-gather(bf16[128,960]{0,1:T(8,128)(2,1)S(1)} %copy-done.18), channel_id=1, replica_groups=mesh['dp'=4,'gx'=2,'gy'=4] {'dp'}, dimensions={0}, use_global_device_ids=true | all-gather | bytes 1228800 | tf_op jit(solution)/shard_map/all_gather | solution.py:260
  114.6 24.4 %all-gather.12.cloned.1.call-done = bf16[8,320,240]{2,1,0:T(8,128)(2,1)} async-done(((bf16[1,320,240]{2,1,0:T(8,128)(2,1)}), bf16[8,320,240]{2,1,0:T(8,128)(2,1)}) %all-gather.12.cloned.1.call-update) | async-done | bytes 1228816 | tf_op jit(solution)/shard_map/all_gather | solution.py:79
  139.0 2.3 copy.179
  141.3 2.1 reshape.312
  143.4 51.5 %all-gather.18.cloned.1.call-done = bf16[2560,480]{1,0:T(8,128)(2,1)} async-done(((bf16[320,480]{1,0:T(8,128)(2,1)}), bf16[2560,480]{1,0:T(8,128)(2,1)}) %all-gather.18.cloned.1.call-update) | async-done | bytes 2457616 | tf_op jit(solution)/shard_map/all_gather | solution.py:79
  194.9 5.9 copy.137
  200.8 5.7 reshape.309
  206.6 4.5 fusion.61
  211.0 2.8 copy.132
  213.8 3.9 reshape.299
  219.3 2.9 copy.134
  222.2 5.0 reshape.303
  227.3 10.2 %all-gather.10.cloned.1.call-done = bf16[1024,640]{0,1:T(8,128)(2,1)} async-done(((bf16[128,640]{0,1:T(8,128)(2,1)}), bf16[1024,640]{0,1:T(8,128)(2,1)}) %all-gather.10.cloned.1.call-update) | async-done | bytes 1310736 | tf_op jit(solution)/shard_map/all_gather | solution.py:249
  240.3 1.6 exponential_reduce_fusion
  241.9 1.5 copy-done
  243.4 2.0 convolution_convert_fusion.12
  246.6 9.7 %all_gather.36 = bf16[512,960]{0,1:T(8,128)(2,1)S(1)} all-gather(bf16[128,960]{0,1:T(8,128)(2,1)S(1)} %multiply_convert_fusion), channel_id=1, replica_groups=mesh['dp'=4,'gx'=2,'gy'=4] {'dp'}, dimensions={0}, use_global_device_ids=true | all-gather | bytes 1228800 | tf_op jit(solution)/shard_map/all_gather | solution.py:261
  256.3 1.6 convolution_convert_fusion.1
  260.7 2.4 convolution_convert_fusion.5
  263.2 2.3 copy.172
  265.9 3.7 convolution_convert_fusion.6
  269.6 2.3 copy.170
  272.0 16.0 %reduce-scatter.24.cloned.1.call-done = bf16[128,960]{1,0:T(8,128)(2,1)} async-done(((bf16[512,960]{1,0:T(8,128)(2,1)}), bf16[128,960]{1,0:T(8,128)(2,1)}) %reduce-scatter.24.cloned.1.call-update) | async-done | bytes 245776
  289.5 26.3 %reduce-scatter.22.cloned.1.call-done = bf16[128,960]{1,0:T(8,128)(2,1)} async-done(((bf16[512,960]{1,0:T(8,128)(2,1)}), bf16[128,960]{1,0:T(8,128)(2,1)}) %reduce-scatter.22.cloned.1.call-update) | async-done | bytes 245776
  315.7 1.8 copy.171
  317.5 2.3 fusion.29
  319.8 2.3 convolution_convert_fusion.9
  322.2 5.4 fusion.6
  327.6 2.8 fusion.1
  333.4 2.5 copy.174
  336.0 2.0 convolution_convert_fusion.3
  338.0 6.0 reshape.317
  344.0 3.2 copy.144
  347.4 3.1 convolution_multiply_fusion
  350.6 2.1 convolution_convert_fusion.2
  352.7 6.1 reshape.319
  358.7 3.1 copy.145
  361.9 39.3 %reduce-scatter.26.cloned.1.call-done = bf16[128,640]{1,0:T(8,128)(2,1)} async-done(((bf16[1024,640]{1,0:T(8,128)(2,1)}), bf16[128,640]{1,0:T(8,128)(2,1)}) %reduce-scatter.26.cloned.1.call-update) | async-done | bytes 163856
  403.6 3.5 reshape.321
  407.1 3.5 copy.146
  412.1 3.5 reshape.323
  415.6 3.6 copy.147
  419.1 3.7 pad_maximum_fusion.1
  423.1 4.5 convolution_convert_fusion
  427.6 4.4 copy.148
  432.0 5.8 reshape.325
  437.9 3.9 copy.149
  441.7 2.1 convolution_convert_fusion.4
  443.8 4.4 reshape.350
  448.2 5.1 copy.169
  453.3 1.6 copy.151
  455.5 3.1 pad_maximum_fusion
  458.6 12.5 %reduce-scatter.14.cloned.1.call-done = bf16[1,480,240]{2,1,0:T(8,128)(2,1)} async-done(((bf16[8,480,240]{2,1,0:T(8,128)(2,1)}), bf16[1,480,240]{2,1,0:T(8,128)(2,1)}) %reduce-scatter.14.cloned.1.call-update) | async-done | bytes 230416 | tf_op jit(solution)/shard_map/reduce_scatter | solution.py:99
  471.1 69.8 %reduce-scatter.16.cloned.1.call-done = bf16[1,480,240]{2,1,0:T(8,128)(2,1)} async-done(((bf16[8,480,240]{2,1,0:T(8,128)(2,1)}), bf16[1,480,240]{2,1,0:T(8,128)(2,1)}) %reduce-scatter.16.cloned.1.call-update) | async-done | bytes 230416 | tf_op jit(solution)/shard_map/reduce_scatter | solution.py:99
  540.9 69.8 %reduce-scatter.18.cloned.1.call-done = bf16[1,480,160]{2,1,0:T(8,128)(2,1)} async-done(((bf16[8,480,160]{2,1,0:T(8,128)(2,1)}), bf16[1,480,160]{2,1,0:T(8,128)(2,1)}) %reduce-scatter.18.cloned.1.call-update) | async-done | bytes 153616 | tf_op jit(solution)/shard_map/reduce_scatter | solution.py:99
  610.7 2.3 pad_maximum_fusion.7
  613.1 85.0 %reduce-scatter.20.cloned.1.call-done = bf16[1,320,720]{2,1,0:T(8,128)(2,1)} async-done(((bf16[8,320,720]{2,1,0:T(8,128)(2,1)}), bf16[1,320,720]{2,1,0:T(8,128)(2,1)}) %reduce-scatter.20.cloned.1.call-update) | async-done | bytes 460816 | tf_op jit(solution)/shard_map/reduce_scatter | solution.py:99
  698.1 1.5 fusion.68
  699.6 1.6 fusion.41
  702.7 69.5 %all-gather.3 = f32[32,2,960]{2,1,0:T(2,128)S(1)} all-gather(f32[1,2,960]{2,1,0:T(2,128)S(1)} %maximum_bitcast_fusion), channel_id=4, replica_groups=mesh['dp'=4,'gx'=2,'gy'=4] {'dp','gx','gy'}, dimensions={0}, use_global_device_ids=true | all-gather | bytes 253440 | tf_op jit(solution)/shard_map/all_gather | solution.py:345
  773.0 1.9 fusion.36
  (172 shorter events, 42.6 us)
Async XLA Ops:
  7.2 4.5 copy-start.24
  7.2 89.1 %all-gather.16.cloned.1.call-start = ((), (), s32[]{:S(2)}) async-start(), calls=%async_computation.15 | async-start | bytes 5529600 | tf_op jit(solution)/shard_map/all_gather | solution.py:79
  8.3 4.4 copy-start.25
  11.6 1.4 copy-start.26
  11.7 127.3 %all-gather.12.cloned.1.call-start = ((), (), s32[]{:S(2)}) async-start(), calls=%async_computation.8 | async-start | bytes 1474560 | tf_op jit(solution)/shard_map/all_gather | solution.py:79
  12.7 1.5 copy-start.3
  12.7 182.2 %all-gather.18.cloned.1.call-start = ((), (), s32[]{:S(2)}) async-start(), calls=%async_computation.16 | async-start | bytes 2949120 | tf_op jit(solution)/shard_map/all_gather | solution.py:79
  14.1 223.4 %all-gather.10.cloned.1.call-start = ((), (), s32[]{:S(2)}) async-start(), calls=%async_computation.7 | async-start | bytes 1474560 | tf_op jit(solution)/shard_map/all_gather | solution.py:249
  99.2 1.4 copy-start.28
  100.6 0.9 copy-start.9
  102.2 1.9 copy-start.30
  102.2 2.2 copy-start.18
  102.9 36.1 %copy-start.10 = (bf16[960,320]{0,1:T(8,128)(2,1)}, bf16[960,320]{0,1:T(8,128)(2,1)S(1)}, u32[]{:S(2)}) copy-start(bf16[960,320]{0,1:T(8,128)(2,1)S(1)} %reshape.295) | copy-start | bytes 1843204
  104.1 183.9 %reduce-scatter.24.cloned.1.call-start = ((), (), s32[]{:S(2)}) async-start(), calls=%async_computation.18 | async-start | bytes 1310720
  104.4 137.5 %copy-start.16 = (pred[128,1024]{0,1:T(8,128)(4,1)}, pred[128,1024]{0,1:T(8,128)(4,1)S(1)}, u32[]{:S(2)}) copy-start(pred[128,1024]{0,1:T(8,128)(4,1)S(1)} %fusion.26) | copy-start | bytes 393220
  217.7 1.5 copy-start.5
  238.9 1.4 copy-start.6
  238.9 3.0 copy-start.22
  240.3 3.1 copy-start
  243.4 2.0 copy-start.2
  245.4 10.8 %copy-start.12 = (bf16[5,64,3,128]{3,1,2,0:T(8,128)(2,1)}, bf16[5,64,3,128]{3,1,2,0:T(8,128)(2,1)S(1)}, u32[]{:S(2)}) copy-start(bf16[5,64,3,128]{3,1,2,0:T(8,128)(2,1)S(1)} %convolution_convert_fusion.12) | copy-start | bytes 737284
  245.4 1.0 copy-start.29
  245.4 10.8 %copy-start.8 = (bf16[1280,960]{1,0:T(8,128)(2,1)S(1)}, bf16[1280,960]{1,0:T(8,128)(2,1)}, u32[]{:S(2)}) copy-start(bf16[1280,960]{1,0:T(8,128)(2,1)} %reshape.309) | copy-start | bytes 7372804
  256.2 1.6 copy-start.21
  256.2 1.7 copy-start.15
  256.2 1.9 copy-start.19
  258.2 1.4 copy-start.33
  259.6 0.9 copy-start.31
  259.6 1.1 copy-start.32
  265.5 50.3 %reduce-scatter.22.cloned.1.call-start = ((), (), s32[]{:S(2)}) async-start(), calls=%async_computation.17 | async-start | bytes 1310720
  271.9 129.3 %reduce-scatter.26.cloned.1.call-start = ((), (), s32[]{:S(2)}) async-start(), calls=%async_computation.19 | async-start | bytes 1474560
  289.1 26.6 %copy-start.11 = (bf16[128,960]{0,1:T(8,128)(2,1)}, bf16[128,960]{0,1:T(8,128)(2,1)S(1)}, u32[]{:S(2)}) copy-start(bf16[128,960]{0,1:T(8,128)(2,1)S(1)} %copy.173) | copy-start | bytes 737284
  317.5 4.5 copy-start.13
  317.5 10.0 %slice-start = ((s8[7864320]{0:T(1024)(128)(4,1)}), s8[4194304]{0:T(1024)(128)(4,1)S(1)}, s32[]{:S(2)}) async-start(s8[7864320]{0:T(1024)(128)(4,1)} %bitcast.180), calls=%async_computation.20 | async-start | bytes 8388608
  319.8 2.4 copy-start.17
  322.2 5.4 slice-start.1
  322.2 5.4 copy-start.23
  330.4 1.9 copy-start.1
  333.4 2.5 copy-start.14
  335.9 135.2 %reduce-scatter.14.cloned.1.call-start = ((), (), s32[]{:S(2)}) async-start(), calls=%async_computation.9 | async-start | bytes 2211840 | tf_op jit(solution)/shard_map/reduce_scatter | solution.py:99
  347.2 193.7 %reduce-scatter.16.cloned.1.call-start = ((), (), s32[]{:S(2)}) async-start(), calls=%async_computation.10 | async-start | bytes 2211840 | tf_op jit(solution)/shard_map/reduce_scatter | solution.py:99
  361.9 248.8 %reduce-scatter.18.cloned.1.call-start = ((), (), s32[]{:S(2)}) async-start(), calls=%async_computation.11 | async-start | bytes 2211840 | tf_op jit(solution)/shard_map/reduce_scatter | solution.py:99
  402.3 8.3 %copy-start.27 = (bf16[128,640]{1,0:T(8,128)(2,1)S(1)}, bf16[128,640]{1,0:T(8,128)(2,1)}, u32[]{:S(2)}) copy-start(bf16[128,640]{1,0:T(8,128)(2,1)} %reduce-scatter.26.cloned.1.call-done) | copy-start | bytes 491524
  422.8 275.2 %reduce-scatter.20.cloned.1.call-start = ((), (), s32[]{:S(2)}) async-start(), calls=%async_computation.13 | async-start | bytes 4423680 | tf_op jit(solution)/shard_map/reduce_scatter | solution.py:99
  437.8 3.9 copy-start.20
  437.9 3.9 copy-start.34
  453.3 2.1 copy-start.4
  458.6 316.3 %all-reduce.2.cloned.1.call-start = ((), (), s32[]{:S(2)}) async-start(), calls=%async_computation.12 | async-start | bytes 1228800 | tf_op jit(solution)/shard_map/psum | solution.py:349
  613.0 165.7 %all-gather.14.cloned.1.call-start = ((), (), s32[]{:S(2)}) async-start(), calls=%async_computation.14 | async-start | bytes 2457600 | tf_op jit(solution)/shard_map/all_gather | solution.py:296
  774.9 2.8 copy-start.7
Sparse Core Ops, SparseCore 0:
  11.8 84.5 all-gather.15
  99.0 39.9 all-gather.11
  141.6 53.2 all-gather.17
  197.3 40.1 all-gather.9
  265.6 22.3 reduce-scatter.23
  290.9 24.7 reduce-scatter.21
  336.1 65.1 reduce-scatter.25
  404.7 66.4 reduce-scatter.13
  474.6 66.2 reduce-scatter.15
  544.2 66.4 reduce-scatter.17
  614.4 83.6 reduce-scatter.19
  700.9 33.4 all-reduce.1
  735.9 22.0 all-gather.13
where the time goes:
time: 800 us; the launch traced here: 793 us
  waiting for transfers between devices  487 us (61%)
  local copies, waits for them, and re-layouts  131 us (16%)
  blocking collectives  89.3 us (11%)
  matrix products  48.1 us (6%)
  other arithmetic  21.8 us (3%)
  between operations  14.9 us (2%)
    reduce_scatter x4, waiting for transfers between devices, scatter_blocks(): lax.psum_scatter(blocks, ('gx', 'gy'), scatter_dimension=0, tiled=False)  237 us
    all_gather x3, waiting for transfers between devices, gather_blocks(): return lax.all_gather(block, ('gx', 'gy'), axis=0, tiled=False)  158 us
    unnamed x16, waiting for transfers between devices  81.7 us
    all_gather x1, blocking collectives, on_device(): lax.all_gather(jnp.stack([attgain_part, mlpgain_part]), ('dp', 'gx', 'gy'...  69.5 us
    reshape x6, local copies, waits for them, and re-layouts, cut_blocks(): grad.astype(jnp.bfloat16).reshape(fanin, rows, fanout, columns)  28.6 us
    unnamed x90, local copies, waits for them, and re-layouts  23.7 us
  transfers between devices with their start and end apart: 13, of which 11 were waited for; matrix products, arithmetic and copies ran while one was open for 19% of the time, Pallas kernels for 0%

commit v1 on v0

--- a/solution.py
+++ b/solution.py
@@ -10,6 +10,12 @@
 THETA = 100000.0
 EPSILON = 1e-05
 MASKED = -1e30
+
+
+def touch_circles(vector, here_x):
+    y = jnp.concatenate([vector, here_x], 1)
+    raw_out = lax.all_gather(y, "dp", axis=0, tiled=True)
+    return jnp.split(raw_out, [vector.shape[1]], 1)
 
 
 def rope_angles(positions):
@@ -257,8 +263,7 @@
     )
     hidden = residual + attn_out.astype(jnp.float32)
     rms_two, unit_two, normed_two = normalize(hidden, mlp_gain)
-    cot_all = lax.all_gather(cotangent, "dp", axis=0, tiled=True)
-    normed_all = lax.all_gather(normed_two, "dp", axis=0, tiled=True)
+    cot_all, normed_all = touch_circles(cotangent, here_x=normed_two)
     gate_up = back_product(normed_all, gate_up_rows).astype(jnp.bfloat16)
     gate_float = gate_up[:, :hidden_width].astype(jnp.float32)
     up_float = gate_up[:, hidden_width:].astype(jnp.float32)

time: 800 us -> 815 us (1.019)
  waiting for transfers between devices: 487 us -> 513 us
  blocking collectives: 89.3 us -> 69.5 us
    all_gather x2 -> x0, blocking collectives: 19.8 us -> none  [the longest x1 10.1 us: on_device(): cot_all = lax.all_gather(cotangent, 'dp', axis=0, tiled=True)]
    all_gather x0 -> x1, waiting for transfers between devices: none -> 10.8 us  [touch_circles(): raw_out = lax.all_gather(y, 'dp', axis=0, tiled=True)]
    unnamed x16 -> x17, waiting for transfers between devices: 81.7 us -> 84.2 us
    unnamed x90 -> x86, local copies, waits for them, and re-layouts: 23.7 us -> 24.3 us
  transfers between devices with their start and end apart: 13 -> 14, of which waited for: 11 -> 12; matrix products, arithmetic and copies ran while one was open for 19% -> 19% of each run, Pallas kernels for 0% -> 0%
where the time goes in v1:
time: 815 us; the launch traced here: 807 us
  waiting for transfers between devices  513 us (63%)
  local copies, waits for them, and re-layouts  135 us (17%)
  blocking collectives  69.5 us (9%)
  matrix products  50.4 us (6%)
  other arithmetic  22.4 us (3%)
  between operations  14.9 us (2%)
    reduce_scatter x4, waiting for transfers between devices, scatter_blocks(): lax.psum_scatter(blocks, ('gx', 'gy'), scatter_dimension=0, tiled=False)  237 us
    all_gather x3, waiting for transfers between devices, gather_blocks(): return lax.all_gather(block, ('gx', 'gy'), axis=0, tiled=False)  166 us
    unnamed x17, waiting for transfers between devices  84.2 us
    all_gather x1, blocking collectives, on_device(): lax.all_gather(jnp.stack([attgain_part, mlpgain_part]), ('dp', 'gx', 'gy'...  69.5 us
    reshape x6, local copies, waits for them, and re-layouts, cut_blocks(): grad.astype(jnp.bfloat16).reshape(fanin, rows, fanout, columns)  28.6 us
    unnamed x86, local copies, waits for them, and re-layouts  24.3 us
  transfers between devices with their start and end apart: 14, of which 12 were waited for; matrix products, arithmetic and copies ran while one was open for 19% of the time, Pallas kernels for 0%

profile of v1, /device:TPU:0, one launch (start us, length us, event | category | flops | bytes accessed | tf_op | source)
XLA Modules:
  0.0 806.9 jit_solution(106580712702877046)
XLA Ops:
  9.4 2.2 pad_maximum_fusion.6
  12.0 84.3 %all-gather.19.cloned.1.call-done = bf16[3840,640]{1,0:T(8,128)(2,1)} async-done(((bf16[480,640]{1,0:T(8,128)(2,1)}), bf16[3840,640]{1,0:T(8,128)(2,1)}) %all-gather.19.cloned.1.call-update) | async-done | bytes 4915216 | tf_op jit(solution)/shard_map/all_gather | solution.py:85
  96.3 2.8 fusion.67
  107.9 4.6 fusion.66
  112.4 2.8 copy.128
  115.3 4.1 reshape.299
  120.9 2.8 copy.130
  123.7 4.8 reshape.303
  128.7 15.3 %all-gather.11.cloned.1.call-done = bf16[1024,640]{0,1:T(8,128)(2,1)} async-done(((bf16[128,640]{0,1:T(8,128)(2,1)}), bf16[1024,640]{0,1:T(8,128)(2,1)}) %all-gather.11.cloned.1.call-update) | async-done | bytes 1310736 | tf_op jit(solution)/shard_map/all_gather | solution.py:255
  146.8 1.6 exponential_reduce_fusion
  149.8 2.0 convolution_convert_fusion.12
  154.1 32.8 %all-gather.15.cloned.1.call-done = bf16[8,320,240]{2,1,0:T(8,128)(2,1)} async-done(((bf16[1,320,240]{2,1,0:T(8,128)(2,1)}), bf16[8,320,240]{2,1,0:T(8,128)(2,1)}) %all-gather.15.cloned.1.call-update) | async-done | bytes 1228816 | tf_op jit(solution)/shard_map/all_gather | solution.py:85
  186.9 3.4 copy.173
  190.2 3.9 reshape.312
  194.2 48.5 %all-gather.21.cloned.1.call-done = bf16[2560,480]{1,0:T(8,128)(2,1)} async-done(((bf16[320,480]{1,0:T(8,128)(2,1)}), bf16[2560,480]{1,0:T(8,128)(2,1)}) %all-gather.21.cloned.1.call-update) | async-done | bytes 2457616 | tf_op jit(solution)/shard_map/all_gather | solution.py:85
  242.7 6.1 copy.133
  248.7 5.8 reshape.309
  254.5 10.8 %all-gather.13.cloned.1.call-done = bf16[512,1920]{0,1:T(8,128)(2,1)} async-done(((bf16[128,1920]{0,1:T(8,128)(2,1)}), bf16[512,1920]{0,1:T(8,128)(2,1)}) %all-gather.13.cloned.1.call-update) | async-done | bytes 1966096 | tf_op jit(solution)/shard_map/all_gather | solution.py:17
  265.3 3.8 convolution_convert_fusion.1
  271.6 2.4 convolution_convert_fusion.5
  274.1 2.3 copy.166
  276.4 3.7 convolution_convert_fusion.6
  280.1 2.3 copy.164
  282.9 18.4 %reduce-scatter.24.cloned.1.call-done = bf16[128,960]{1,0:T(8,128)(2,1)} async-done(((bf16[512,960]{1,0:T(8,128)(2,1)}), bf16[128,960]{1,0:T(8,128)(2,1)}) %reduce-scatter.24.cloned.1.call-update) | async-done | bytes 245776
  302.8 26.4 %reduce-scatter.22.cloned.1.call-done = bf16[128,960]{1,0:T(8,128)(2,1)} async-done(((bf16[512,960]{1,0:T(8,128)(2,1)}), bf16[128,960]{1,0:T(8,128)(2,1)}) %reduce-scatter.22.cloned.1.call-update) | async-done | bytes 245776
  329.2 1.8 copy.165
  331.0 2.3 fusion.34
  333.3 2.3 convolution_convert_fusion.9
  335.7 5.4 fusion.6
  341.1 2.8 fusion.1
  346.9 2.5 copy.168
  349.5 2.0 convolution_convert_fusion.3
  351.5 6.0 reshape.317
  357.5 3.1 copy.139
  360.6 3.1 convolution_multiply_fusion
  363.8 2.1 convolution_convert_fusion.2
  365.9 6.0 reshape.319
  372.0 3.2 copy.140
  375.4 39.2 %reduce-scatter.26.cloned.1.call-done = bf16[128,640]{1,0:T(8,128)(2,1)} async-done(((bf16[1024,640]{1,0:T(8,128)(2,1)}), bf16[128,640]{1,0:T(8,128)(2,1)}) %reduce-scatter.26.cloned.1.call-update) | async-done | bytes 163856
  417.0 3.5 reshape.321
  420.5 3.5 copy.141
  425.4 3.5 reshape.323
  428.9 3.6 copy.142
  432.5 3.6 pad_maximum_fusion.1
  436.2 4.6 convolution_convert_fusion
  440.7 4.5 copy.143
  445.3 5.8 reshape.325
  451.1 3.9 copy.144
  455.0 2.1 convolution_convert_fusion.4
  457.1 4.4 reshape.350
  461.5 5.2 copy.163
  466.7 1.6 copy.146
  468.8 3.0 pad_maximum_fusion
  471.8 12.7 %reduce-scatter.14.cloned.1.call-done = bf16[1,480,240]{2,1,0:T(8,128)(2,1)} async-done(((bf16[8,480,240]{2,1,0:T(8,128)(2,1)}), bf16[1,480,240]{2,1,0:T(8,128)(2,1)}) %reduce-scatter.14.cloned.1.call-update) | async-done | bytes 230416 | tf_op jit(solution)/shard_map/reduce_scatter | solution.py:105
  484.6 70.0 %reduce-scatter.16.cloned.1.call-done = bf16[1,480,240]{2,1,0:T(8,128)(2,1)} async-done(((bf16[8,480,240]{2,1,0:T(8,128)(2,1)}), bf16[1,480,240]{2,1,0:T(8,128)(2,1)}) %reduce-scatter.16.cloned.1.call-update) | async-done | bytes 230416 | tf_op jit(solution)/shard_map/reduce_scatter | solution.py:105
  554.5 70.1 %reduce-scatter.18.cloned.1.call-done = bf16[1,480,160]{2,1,0:T(8,128)(2,1)} async-done(((bf16[8,480,160]{2,1,0:T(8,128)(2,1)}), bf16[1,480,160]{2,1,0:T(8,128)(2,1)}) %reduce-scatter.18.cloned.1.call-update) | async-done | bytes 153616 | tf_op jit(solution)/shard_map/reduce_scatter | solution.py:105
  624.7 2.3 pad_maximum_fusion.7
  627.2 84.5 %reduce-scatter.20.cloned.1.call-done = bf16[1,320,720]{2,1,0:T(8,128)(2,1)} async-done(((bf16[8,320,720]{2,1,0:T(8,128)(2,1)}), bf16[1,320,720]{2,1,0:T(8,128)(2,1)}) %reduce-scatter.20.cloned.1.call-update) | async-done | bytes 460816 | tf_op jit(solution)/shard_map/reduce_scatter | solution.py:105
  711.8 1.5 fusion.73
  713.3 1.6 fusion.46
  714.9 1.5 fusion.42
  716.4 69.5 %all-gather.3 = f32[32,2,960]{2,1,0:T(2,128)S(1)} all-gather(f32[1,2,960]{2,1,0:T(2,128)S(1)} %maximum_bitcast_fusion), channel_id=4, replica_groups=mesh['dp'=4,'gx'=2,'gy'=4] {'dp','gx','gy'}, dimensions={0}, use_global_device_ids=true | all-gather | bytes 253440 | tf_op jit(solution)/shard_map/all_gather | solution.py:350
  786.6 1.9 fusion.41
  792.4 1.5 slice.127
  (170 shorter events, 42.7 us)
Async XLA Ops:
  7.2 4.5 copy-start.3
  7.2 89.1 %all-gather.19.cloned.1.call-start = ((), (), s32[]{:S(2)}) async-start(), calls=%async_computation.16 | async-start | bytes 5529600 | tf_op jit(solution)/shard_map/all_gather | solution.py:85
  11.6 132.4 %all-gather.11.cloned.1.call-start = ((), (), s32[]{:S(2)}) async-start(), calls=%async_computation.7 | async-start | bytes 1474560 | tf_op jit(solution)/shard_map/all_gather | solution.py:255
  99.1 1.4 copy-start.24
  100.5 0.8 copy-start.9
  102.1 1.9 copy-start.21
  102.8 2.6 copy-start.10
  102.8 2.3 copy-start.22
  104.0 82.9 %all-gather.15.cloned.1.call-start = ((), (), s32[]{:S(2)}) async-start(), calls=%async_computation.9 | async-start | bytes 1474560 | tf_op jit(solution)/shard_map/all_gather | solution.py:85
  105.0 2.6 copy-start.26
  105.0 137.6 %all-gather.21.cloned.1.call-start = ((), (), s32[]{:S(2)}) async-start(), calls=%async_computation.17 | async-start | bytes 2949120 | tf_op jit(solution)/shard_map/all_gather | solution.py:85
  107.5 157.8 %all-gather.13.cloned.1.call-start = ((), (), s32[]{:S(2)}) async-start(), calls=%async_computation.8 | async-start | bytes 2457600 | tf_op jit(solution)/shard_map/all_gather | solution.py:17
  107.9 40.5 %copy-start.16 = (pred[128,1024]{0,1:T(8,128)(4,1)}, pred[128,1024]{0,1:T(8,128)(4,1)S(1)}, u32[]{:S(2)}) copy-start(pred[128,1024]{0,1:T(8,128)(4,1)S(1)} %fusion.31) | copy-start | bytes 393220
  119.3 1.6 copy-start.5
  145.4 1.4 copy-start.6
  145.4 3.0 copy-start.19
  146.8 3.1 copy-start
  149.8 2.0 copy-start.2
  151.8 2.0 copy-start.12
  151.8 1.0 copy-start.25
  151.8 1.2 copy-start.18
  153.8 147.5 %reduce-scatter.24.cloned.1.call-start = ((), (), s32[]{:S(2)}) async-start(), calls=%async_computation.19 | async-start | bytes 1310720
  265.3 3.8 copy-start.15
  265.3 3.8 copy-start.27
  269.1 1.4 copy-start.31
  269.1 2.5 copy-start.8
  270.5 0.8 copy-start.29
  270.5 1.1 copy-start.30
  276.3 52.9 %reduce-scatter.22.cloned.1.call-start = ((), (), s32[]{:S(2)}) async-start(), calls=%async_computation.18 | async-start | bytes 1310720
  282.4 132.2 %reduce-scatter.26.cloned.1.call-start = ((), (), s32[]{:S(2)}) async-start(), calls=%async_computation.20 | async-start | bytes 1474560
  302.4 26.8 %copy-start.11 = (bf16[128,960]{0,1:T(8,128)(2,1)}, bf16[128,960]{0,1:T(8,128)(2,1)S(1)}, u32[]{:S(2)}) copy-start(bf16[128,960]{0,1:T(8,128)(2,1)S(1)} %copy.167) | copy-start | bytes 737284
  331.0 4.5 copy-start.13
  331.0 10.0 %slice-start = ((s8[7864320]{0:T(1024)(128)(4,1)}), s8[4194304]{0:T(1024)(128)(4,1)S(1)}, s32[]{:S(2)}) async-start(s8[7864320]{0:T(1024)(128)(4,1)} %bitcast.174), calls=%async_computation.21 | async-start | bytes 8388608
  333.3 2.4 copy-start.17
  335.6 5.4 slice-start.1
  335.6 5.4 copy-start.20
  343.8 1.9 copy-start.1
  346.9 2.6 copy-start.14
  349.4 135.2 %reduce-scatter.14.cloned.1.call-start = ((), (), s32[]{:S(2)}) async-start(), calls=%async_computation.10 | async-start | bytes 2211840 | tf_op jit(solution)/shard_map/reduce_scatter | solution.py:105
  360.6 193.9 %reduce-scatter.16.cloned.1.call-start = ((), (), s32[]{:S(2)}) async-start(), calls=%async_computation.11 | async-start | bytes 2211840 | tf_op jit(solution)/shard_map/reduce_scatter | solution.py:105
  375.2 249.5 %reduce-scatter.18.cloned.1.call-start = ((), (), s32[]{:S(2)}) async-start(), calls=%async_computation.12 | async-start | bytes 2211840 | tf_op jit(solution)/shard_map/reduce_scatter | solution.py:105
  415.7 8.3 %copy-start.23 = (bf16[128,640]{1,0:T(8,128)(2,1)S(1)}, bf16[128,640]{1,0:T(8,128)(2,1)}, u32[]{:S(2)}) copy-start(bf16[128,640]{1,0:T(8,128)(2,1)} %reduce-scatter.26.cloned.1.call-done) | copy-start | bytes 491524
  436.1 275.6 %reduce-scatter.20.cloned.1.call-start = ((), (), s32[]{:S(2)}) async-start(), calls=%async_computation.14 | async-start | bytes 4423680 | tf_op jit(solution)/shard_map/reduce_scatter | solution.py:105
  451.1 3.9 copy-start.28
  451.1 3.9 copy-start.32
  466.7 2.1 copy-start.4
  471.8 316.7 %all-reduce.2.cloned.1.call-start = ((), (), s32[]{:S(2)}) async-start(), calls=%async_computation.13 | async-start | bytes 1228800 | tf_op jit(solution)/shard_map/psum | solution.py:354
  627.0 165.4 %all-gather.17.cloned.1.call-start = ((), (), s32[]{:S(2)}) async-start(), calls=%async_computation.15 | async-start | bytes 2457600 | tf_op jit(solution)/shard_map/all_gather | solution.py:301
  788.5 2.8 copy-start.7
Sparse Core Ops, SparseCore 0:
  11.7 84.5 all-gather.18
  104.1 39.8 all-gather.10
  146.7 40.1 all-gather.14
  189.4 53.2 all-gather.20
  244.6 20.6 all-gather.12
  276.5 24.7 reduce-scatter.23
  304.4 24.7 reduce-scatter.21
  349.5 65.0 reduce-scatter.25
  418.1 66.4 reduce-scatter.13
  487.9 66.6 reduce-scatter.15
  558.0 66.6 reduce-scatter.17
  628.2 83.5 reduce-scatter.19
  714.7 33.4 all-reduce.1
  749.7 21.9 all-gather.16
